TPU v7x, 32 devices: a whole 2x2x4 slice. The times are simulated.
32 devices in a mesh: seq: 8 (over z, x), head: 4 (over y, core).
Axes of the slice: x: 2, y: 2, z: 4, core: 2. Of those that a mesh axis runs over, the one named last changes fastest.
Arguments:
- context: bfloat16 [16384, 2048], P('seq'), may hold values from -64 to 64
- wq_cross: bfloat16 [2048, 2048], P(None, 'head'), may hold values from -4 to 4
- wk_cross: bfloat16 [2048, 2048], P(None, 'head'), may hold values from -4 to 4
- wv_cross: bfloat16 [2048, 2048], P(None, 'head'), may hold values from -0.125 to 0.125
- wo_cross: bfloat16 [2048, 2048], P('head'), may hold values from -0.125 to 0.125
- wq_latent: bfloat16 [2048, 2048], P(None, 'head'), may hold values from -4 to 4
- wk_latent: bfloat16 [2048, 2048], P(None, 'head'), may hold values from -4 to 4
- wv_latent: bfloat16 [2048, 2048], P(None, 'head'), may hold values from -0.125 to 0.125
- wo_latent: bfloat16 [2048, 2048], P('head'), may hold values from -0.125 to 0.125
- cross_keep: int32 [16, 2048, 2048], P('head', None, 'seq'), may hold values from 0 to 255, as said below
- latent_keep: int32 [16, 2048, 128], P('head'), may hold values from 0 to 65535, as said below
- residual_keep: int32 [2, 2048, 128], replicated, may hold values from 0 to 65535, as said below
Outputs:
- latents_out: bfloat16 [2048, 2048], P('seq', 'head')
Inputs may be any that keep to these rules, and one draw needn't show every extreme that they name: `cross_keep`: each of the 8 low bits of a word is one keep flag, laid out as the steps say. `latent_keep`: each of the 16 low bits of a word is one keep flag, laid out as the steps say. `residual_keep`: each of the 16 low bits of a word is one keep flag, laid out as the steps say.
All inputs are finite; a program needn't handle non-finite values.
Results may differ from a plain program's by a relative error of at most 0.015.
Values may be sent and summed in bfloat16 or wider, within the bound.
A program may use at most 128 MiB of HBM per device.

v0:
```python
import math
import jax
import jax.numpy as jnp
from jax import lax
from jax.sharding import PartitionSpec as P

keep_scale = 8.0 / 7.0
masked = -1e30


def from_root(value, axis, source):
    kept = jnp.where(lax.axis_index(axis) == source, value, 0).astype(value.dtype)
    return lax.psum(kept, axis)


def unpack_bits(packed_words, word_bits):
    shifts = jnp.arange(word_bits, dtype=jnp.int32)
    bit_table = jnp.bitwise_and(jnp.right_shift(packed_words[..., None, :], shifts[:, None]), 1)
    return bit_table.reshape(packed_words.shape[:-1] + (word_bits * packed_words.shape[-1],))


def rms_rows(matrix):
    wide_rows = matrix.astype(jnp.float32)
    mean_square = jnp.mean(wide_rows * wide_rows, axis=-1, keepdims=True)
    return (wide_rows * lax.rsqrt(mean_square + 1e-06)).astype(jnp.bfloat16)


def per_device(
    context,
    wq_cross,
    wk_cross,
    wv_cross,
    wo_cross,
    wq_latent,
    wk_latent,
    wv_latent,
    wo_latent,
    cross_keep,
    latent_keep,
    residual_keep,
):
    seq_count = lax.axis_size("seq")
    seq_index = lax.axis_index("seq")
    head_index = lax.axis_index("head")
    tok_rows, model_width = context.shape
    head_local = cross_keep.shape[0]
    latent_count = cross_keep.shape[1]
    head_dim = wq_cross.shape[1] // head_local
    query_width = head_local * head_dim
    columns = model_width // lax.axis_size("head")
    local_rows = latent_count // seq_count
    score_scale = 1.0 / math.sqrt(head_dim)
    normed = rms_rows(context)
    key_rows = jnp.dot(normed, wk_cross, preferred_element_type=jnp.float32).astype(jnp.bfloat16)
    value_rows = jnp.dot(normed, wv_cross, preferred_element_type=jnp.float32).astype(jnp.bfloat16)
    own_queries = jnp.dot(normed, wq_cross, preferred_element_type=jnp.float32).astype(jnp.bfloat16)
    own_columns = lax.dynamic_slice_in_dim(context, head_index * columns, columns, 1)
    outgoing_rows = jnp.concatenate([own_queries, own_columns], axis=1)
    arrived_rows = from_root(outgoing_rows, "seq", seq_count - 1)
    queries = arrived_rows[:, :query_width]
    latent_context = arrived_rows[:, query_width:]
    first_latent = (seq_count - 1) * tok_rows
    block_rows = min(512, latent_count)
    block_count = latent_count // block_rows
    query_blocks = queries.reshape(block_count, block_rows, head_local, head_dim)
    mask_blocks = cross_keep.reshape(head_local, block_count, block_rows, -1).transpose(1, 0, 2, 3)
    key_heads = key_rows.reshape(tok_rows, head_local, head_dim)
    value_heads = value_rows.reshape(tok_rows, head_local, head_dim)
    key_pos = seq_index * tok_rows + jnp.arange(tok_rows, dtype=jnp.int32)

    def cross_block(block_items):
        query_block, mask_block, number = block_items
        scores = (
            jnp.einsum("qhd,khd->hqk", query_block, key_heads, preferred_element_type=jnp.float32)
            * score_scale
        )
        query_pos = first_latent + number * block_rows + jnp.arange(block_rows, dtype=jnp.int32)
        allowed = key_pos[None, None, :] <= query_pos[None, :, None]
        scores = jnp.where(allowed, scores, masked)
        row_top = jnp.max(scores, axis=-1)
        exponent = jnp.where(allowed, jnp.exp(scores - row_top[..., None]), 0.0)
        row_sum = jnp.sum(exponent, axis=-1)
        keep_flags = unpack_bits(mask_block, 8).astype(jnp.float32)
        weights = (exponent * keep_flags * keep_scale).astype(jnp.bfloat16)
        summed = jnp.einsum(
            "hqk,khd->hqd", weights, value_heads, preferred_element_type=jnp.float32
        )
        return (summed, row_top, row_sum)

    summed, row_top, row_sum = lax.map(
        cross_block, (query_blocks, mask_blocks, jnp.arange(block_count, dtype=jnp.int32))
    )
    summed = summed.transpose(1, 0, 2, 3).reshape(head_local, latent_count, head_dim)
    row_top = row_top.transpose(1, 0, 2).reshape(head_local, latent_count)
    row_sum = row_sum.transpose(1, 0, 2).reshape(head_local, latent_count)
    first_row = seq_index * local_rows
    row_peak = lax.pmax(row_top, "seq")
    factor = jnp.exp(row_top - row_peak)
    numerator, denominator = (
        lax.psum_scatter(
            (summed * factor[..., None]).astype(jnp.bfloat16),
            "seq",
            scatter_dimension=1,
            tiled=True,
        ).astype(jnp.float32),
        lax.psum_scatter(
            (row_sum * factor).astype(jnp.bfloat16), "seq", scatter_dimension=1, tiled=True
        ).astype(jnp.float32),
    )
    attended_heads = numerator / denominator[..., None]
    attended = (
        attended_heads.transpose(1, 0, 2)
        .reshape(local_rows, head_local * head_dim)
        .astype(jnp.bfloat16)
    )
    inputs = lax.dynamic_slice_in_dim(latent_context, first_row, local_rows, 0).astype(jnp.float32)
    residual_rows = lax.dynamic_slice_in_dim(residual_keep, first_row, local_rows, 1)
    residual_mask = lax.dynamic_slice_in_dim(
        unpack_bits(residual_rows, 16), head_index * columns, columns, 2
    ).astype(jnp.float32)
    branch = jnp.dot(attended, wo_cross, preferred_element_type=jnp.float32)
    branch = lax.psum_scatter(
        branch.astype(jnp.bfloat16), "head", scatter_dimension=1, tiled=True
    ).astype(jnp.float32)
    latents = (inputs + residual_mask[0] * keep_scale * branch).astype(jnp.bfloat16)
    wide_latents = latents.astype(jnp.float32)
    squares = lax.psum(jnp.sum(wide_latents * wide_latents, axis=-1), "head")
    normed_columns = (wide_latents * lax.rsqrt(squares / model_width + 1e-06)[:, None]).astype(
        jnp.bfloat16
    )
    normed_latents = lax.all_gather(normed_columns, "head", axis=1, tiled=True)
    latent_queries = jnp.dot(normed_latents, wq_latent, preferred_element_type=jnp.float32).astype(
        jnp.bfloat16
    )
    latent_keys = jnp.dot(normed_latents, wk_latent, preferred_element_type=jnp.float32).astype(
        jnp.bfloat16
    )
    latent_values = jnp.dot(normed_latents, wv_latent, preferred_element_type=jnp.float32).astype(
        jnp.bfloat16
    )
    my_index = first_row + jnp.arange(local_rows, dtype=jnp.int32)
    latent_words = lax.dynamic_slice_in_dim(latent_keep, first_row, local_rows, 1)
    latent_mask = unpack_bits(latent_words, 16).astype(jnp.float32)
    query_heads = latent_queries.reshape(local_rows, head_local, head_dim)
    initial = (
        jnp.zeros((head_local, local_rows, head_dim), jnp.float32),
        jnp.full((head_local, local_rows), masked, jnp.float32),
        jnp.zeros((head_local, local_rows), jnp.float32),
    )
    key_piece = lax.all_gather(latent_keys, "seq", axis=0, tiled=True)
    value_piece = lax.all_gather(latent_values, "seq", axis=0, tiled=True)
    piece_rows = key_piece.shape[0]
    key_index = jnp.arange(piece_rows, dtype=jnp.int32)

    def update(current):
        weighted, old_top, old_sum = current
        scores = (
            jnp.einsum(
                "qhd,khd->hqk",
                query_heads,
                key_piece.reshape(piece_rows, head_local, head_dim),
                preferred_element_type=jnp.float32,
            )
            * score_scale
        )
        allowed = key_index[None, None, :] <= my_index[None, :, None]
        scores = jnp.where(allowed, scores, masked)
        new_top = jnp.maximum(old_top, jnp.max(scores, axis=-1))
        exponent = jnp.where(allowed, jnp.exp(scores - new_top[..., None]), 0.0)
        keep_flags = jnp.take(latent_mask, key_index, axis=2)
        weights = (exponent * keep_flags * keep_scale).astype(jnp.bfloat16)
        added = jnp.einsum(
            "hqk,khd->hqd",
            weights,
            value_piece.reshape(piece_rows, head_local, head_dim),
            preferred_element_type=jnp.float32,
        )
        return (added, new_top, jnp.sum(exponent, axis=-1))

    needed = jnp.min(key_index) <= jnp.max(my_index)
    weighted, latent_top, latent_sum = lax.cond(needed, update, lambda current: current, initial)
    latent_attended = (
        (weighted / latent_sum[..., None])
        .transpose(1, 0, 2)
        .reshape(local_rows, head_local * head_dim)
        .astype(jnp.bfloat16)
    )
    latent_branch = jnp.dot(latent_attended, wo_latent, preferred_element_type=jnp.float32)
    latent_branch = lax.psum_scatter(
        latent_branch.astype(jnp.bfloat16), "head", scatter_dimension=1, tiled=True
    ).astype(jnp.float32)
    result = (wide_latents + residual_mask[1] * keep_scale * latent_branch).astype(jnp.bfloat16)
    return result


def solution(mesh):
    in_specs = (
        P("seq", None),
        P(None, "head"),
        P(None, "head"),
        P(None, "head"),
        P("head", None),
        P(None, "head"),
        P(None, "head"),
        P(None, "head"),
        P("head", None),
        P("head", None, "seq"),
        P("head", None, None),
        P(),
    )
    out_specs = P("seq", "head")
    return jax.shard_map(
        per_device, mesh=mesh, in_specs=in_specs, out_specs=out_specs, check_vma=False
    )
```

profile of v0, /device:TPU:0, one launch (start us, length us, event | category | flops | bytes accessed | tf_op | source)
XLA Modules:
  0.0 868.4 jit_solution(609139487656249483)
XLA Ops:
  6.5 5.2 fusion.38
  11.8 3.0 constant_dynamic-slice_fusion.2
  14.8 4.0 copy.67
  18.8 9.7 %convolution_convert_fusion.2 = bf16[2048,512]{0,1:T(8,128)(2,1)} fusion(bf16[2048,512]{1,0:T(8,128)(2,1)S(1)} %copy-done, bf16[2048,2048]{1,0:T(8,128)(2,1)} %param.16, f32[2048]{0:T(1024)S(1)} %add_rsqrt_fusion), kind=kOutput, calls=%fused_computation.67 | convolution fusion | flops 4308598784 | bytes 12591104 | tf_op jit(solution)/shard_map/dot_general | solution.py:56
  28.5 4.1 maximum_select_fusion
  33.1 9.0 %convolution_convert_fusion.1 = bf16[2048,512]{0,1:T(8,128)(2,1)S(1)} fusion(bf16[2048,512]{1,0:T(8,128)(2,1)} %param.18, bf16[2048,2048]{1,0:T(8,128)(2,1)} %param.16, f32[2048]{0:T(1024)S(1)} %add_rsqrt_fusion), kind=kOutput, calls=%fused_computation.66 | convolution fusion | flops 4308598784 | bytes 12591104 | tf_op jit(solution)/shard_map/dot_general | solution.py:54
  42.1 2.5 copy.48
  44.6 9.0 %convolution_convert_fusion = bf16[2048,512]{0,1:T(8,128)(2,1)S(1)} fusion(bf16[2048,512]{1,0:T(8,128)(2,1)} %param.19, bf16[2048,2048]{1,0:T(8,128)(2,1)} %param.16, f32[2048]{0:T(1024)S(1)} %add_rsqrt_fusion), kind=kOutput, calls=%fused_computation.65 | convolution fusion | flops 4308598784 | bytes 12591104 | tf_op jit(solution)/shard_map/dot_general | solution.py:55
  53.6 2.5 copy.50
  56.1 135.7 %all-reduce.2.cloned.1.call-done = bf16[2048,1024]{0,1:T(8,128)(2,1)} async-done(((bf16[2048,1024]{0,1:T(8,128)(2,1)}), bf16[2048,1024]{0,1:T(8,128)(2,1)}) %all-reduce.2.cloned.1.call-update) | async-done | bytes 4194320 | tf_op jit(solution)/shard_map/psum | solution.py:13
  191.8 4.8 fusion.60
  196.6 3.3 reshape.146
  199.9 2.9 copy.47
  202.9 254.1 %while.15 = (s32[]{:T(128)}, f32[4,4,512,128]{3,2,0,1:T(8,128)}, f32[4,4,512]{2,1,0:T(4,128)S(1)}, f32[4,4,512]{2,1,0:T(4,128)S(1)}, s32[4]{0:T(128)S(1)}, /*ind...) while((s32[]{:T(128)}, f32[4,4,512,128]{3,2,0,1:T(8,128)}, ...), condition=%wide.region_5.6_spmd.clone, body=%wide.region_2.5_spmd.clone.sunk | while | flops 2224028160 | bytes 142201040 | solution.py:90
  203.0 1.7 dynamic-slice_bitcast_fusion.2
  204.8 7.1 shift_right_arithmetic.115
  211.9 18.0 %shift_right_arithmetic.116 = s32[4,512,2048]{2,1,0:T(8,128)} reshape(s32[4,512,8,256]{3,2,1,0:T(8,128)} %shift_right_arithmetic.115) | data formatting | bytes 33554432 | tf_op jit(solution)/shard_map/while/body/eval_jaxpr/shift_right_arithmetic | solution.py:18
  231.7 10.9 %fusion.86 = (f32[4,512]{1,0:T(4,128)S(1)}, f32[4,512,2048]{2,1,0:T(8,128)}) fusion(pred[512,2048]{1,0:T(8,128)(4,1)S(1)} %broadcast_compare_fusion.3, bf16[2048,4,128]{2,0,1:T(8,128)(2,1)} %get-tuple-element.276, bf16[4,512,4,128]{3,1,2,0:T(8,128)(2,1)} %get-tuple-element.275, s32[]{:T(128)S(6)} %copy.100), kind=kOutput, calls=%fused_computation.33.clone.1 | convolution fusion | flops 1086322688 | bytes 20455428 | tf_op jit(solution)/shard_map/while/body/eval_jaxpr/qhd,khd->hqk/dot_general | solution.py:74
  242.7 15.4 %fusion.87 = f32[4,4,512,128]{3,2,0,1:T(8,128)} fusion(f32[4,4,512,128]{3,2,0,1:T(8,128)} %get-tuple-element.258, s32[]{:T(128)S(6)} %copy.100, bf16[2048,4,128]{2,0,1:T(8,128)(2,1)S(1)} %copy-done.3, s32[4,512,2048]{2,1,0:T(8,128)} %shift_right_arithmetic.116, f32[4,512,2048]{2,1,0:T(8,128)} %get-tuple-element.240, s32[2048]{0:T(1024)S(1)} %bitcast.148, ...), kind=kOutput, calls=%fused_computation.40.clone.1 | convolution fusion | flops 1115684864 | bytes 37765124 | tf_op jit(solution)/shard_map/while/body/eval_jaxpr/hqk,khd->hqd/dot_general | solution.py:85
  258.1 8.4 fusion.88
  266.5 1.7 dynamic-slice_bitcast_fusion.2
  268.2 7.1 shift_right_arithmetic.115
  275.3 18.0 %shift_right_arithmetic.116 = s32[4,512,2048]{2,1,0:T(8,128)} reshape(s32[4,512,8,256]{3,2,1,0:T(8,128)} %shift_right_arithmetic.115) | data formatting | bytes 33554432 | tf_op jit(solution)/shard_map/while/body/eval_jaxpr/shift_right_arithmetic | solution.py:18
  295.2 10.9 %fusion.86 = (f32[4,512]{1,0:T(4,128)S(1)}, f32[4,512,2048]{2,1,0:T(8,128)}) fusion(pred[512,2048]{1,0:T(8,128)(4,1)S(1)} %broadcast_compare_fusion.3, bf16[2048,4,128]{2,0,1:T(8,128)(2,1)} %get-tuple-element.276, bf16[4,512,4,128]{3,1,2,0:T(8,128)(2,1)} %get-tuple-element.275, s32[]{:T(128)S(6)} %copy.100), kind=kOutput, calls=%fused_computation.33.clone.1 | convolution fusion | flops 1086322688 | bytes 20455428 | tf_op jit(solution)/shard_map/while/body/eval_jaxpr/qhd,khd->hqk/dot_general | solution.py:74
  306.1 15.5 %fusion.87 = f32[4,4,512,128]{3,2,0,1:T(8,128)} fusion(f32[4,4,512,128]{3,2,0,1:T(8,128)} %get-tuple-element.258, s32[]{:T(128)S(6)} %copy.100, bf16[2048,4,128]{2,0,1:T(8,128)(2,1)S(1)} %copy-done.3, s32[4,512,2048]{2,1,0:T(8,128)} %shift_right_arithmetic.116, f32[4,512,2048]{2,1,0:T(8,128)} %get-tuple-element.240, s32[2048]{0:T(1024)S(1)} %bitcast.148, ...), kind=kOutput, calls=%fused_computation.40.clone.1 | convolution fusion | flops 1115684864 | bytes 37765124 | tf_op jit(solution)/shard_map/while/body/eval_jaxpr/hqk,khd->hqd/dot_general | solution.py:85
  321.6 8.4 fusion.88
  330.0 1.7 dynamic-slice_bitcast_fusion.2
  331.7 7.1 shift_right_arithmetic.115
  338.9 18.0 %shift_right_arithmetic.116 = s32[4,512,2048]{2,1,0:T(8,128)} reshape(s32[4,512,8,256]{3,2,1,0:T(8,128)} %shift_right_arithmetic.115) | data formatting | bytes 33554432 | tf_op jit(solution)/shard_map/while/body/eval_jaxpr/shift_right_arithmetic | solution.py:18
  358.7 10.9 %fusion.86 = (f32[4,512]{1,0:T(4,128)S(1)}, f32[4,512,2048]{2,1,0:T(8,128)}) fusion(pred[512,2048]{1,0:T(8,128)(4,1)S(1)} %broadcast_compare_fusion.3, bf16[2048,4,128]{2,0,1:T(8,128)(2,1)} %get-tuple-element.276, bf16[4,512,4,128]{3,1,2,0:T(8,128)(2,1)} %get-tuple-element.275, s32[]{:T(128)S(6)} %copy.100), kind=kOutput, calls=%fused_computation.33.clone.1 | convolution fusion | flops 1086322688 | bytes 20455428 | tf_op jit(solution)/shard_map/while/body/eval_jaxpr/qhd,khd->hqk/dot_general | solution.py:74
  369.7 15.4 %fusion.87 = f32[4,4,512,128]{3,2,0,1:T(8,128)} fusion(f32[4,4,512,128]{3,2,0,1:T(8,128)} %get-tuple-element.258, s32[]{:T(128)S(6)} %copy.100, bf16[2048,4,128]{2,0,1:T(8,128)(2,1)S(1)} %copy-done.3, s32[4,512,2048]{2,1,0:T(8,128)} %shift_right_arithmetic.116, f32[4,512,2048]{2,1,0:T(8,128)} %get-tuple-element.240, s32[2048]{0:T(1024)S(1)} %bitcast.148, ...), kind=kOutput, calls=%fused_computation.40.clone.1 | convolution fusion | flops 1115684864 | bytes 37765124 | tf_op jit(solution)/shard_map/while/body/eval_jaxpr/hqk,khd->hqd/dot_general | solution.py:85
  385.1 8.4 fusion.88
  393.5 1.7 dynamic-slice_bitcast_fusion.2
  395.2 7.1 shift_right_arithmetic.115
  402.3 18.0 %shift_right_arithmetic.116 = s32[4,512,2048]{2,1,0:T(8,128)} reshape(s32[4,512,8,256]{3,2,1,0:T(8,128)} %shift_right_arithmetic.115) | data formatting | bytes 33554432 | tf_op jit(solution)/shard_map/while/body/eval_jaxpr/shift_right_arithmetic | solution.py:18
  422.2 10.9 %fusion.86 = (f32[4,512]{1,0:T(4,128)S(1)}, f32[4,512,2048]{2,1,0:T(8,128)}) fusion(pred[512,2048]{1,0:T(8,128)(4,1)S(1)} %broadcast_compare_fusion.3, bf16[2048,4,128]{2,0,1:T(8,128)(2,1)} %get-tuple-element.276, bf16[4,512,4,128]{3,1,2,0:T(8,128)(2,1)} %get-tuple-element.275, s32[]{:T(128)S(6)} %copy.100), kind=kOutput, calls=%fused_computation.33.clone.1 | convolution fusion | flops 1086322688 | bytes 20455428 | tf_op jit(solution)/shard_map/while/body/eval_jaxpr/qhd,khd->hqk/dot_general | solution.py:74
  433.1 15.4 %fusion.87 = f32[4,4,512,128]{3,2,0,1:T(8,128)} fusion(f32[4,4,512,128]{3,2,0,1:T(8,128)} %get-tuple-element.258, s32[]{:T(128)S(6)} %copy.100, bf16[2048,4,128]{2,0,1:T(8,128)(2,1)S(1)} %copy-done.3, s32[4,512,2048]{2,1,0:T(8,128)} %shift_right_arithmetic.116, f32[4,512,2048]{2,1,0:T(8,128)} %get-tuple-element.240, s32[2048]{0:T(1024)S(1)} %bitcast.148, ...), kind=kOutput, calls=%fused_computation.40.clone.1 | convolution fusion | flops 1115684864 | bytes 37765124 | tf_op jit(solution)/shard_map/while/body/eval_jaxpr/hqk,khd->hqd/dot_general | solution.py:85
  448.6 8.4 fusion.88
  457.0 34.9 %pmax.7 = f32[4,2048]{1,0:T(4,128)S(1)} all-reduce(f32[4,2048]{1,0:T(4,128)S(1)} %bitcast.149), channel_id=1, replica_groups=mesh['seq'=8,'head'=4] {'seq'}, use_global_device_ids=true, to_apply=%region_6.7 | all-reduce | flops 8192 | bytes 65536 | tf_op jit(solution)/shard_map/pmax | solution.py:97
  493.0 4.2 fusion.42
  497.2 55.8 %reduce-scatter.13.cloned.1.call-done = bf16[256,4]{1,0:T(8,128)(2,1)} async-done(((bf16[2048,4]{1,0:T(8,128)(2,1)}), bf16[256,4]{1,0:T(8,128)(2,1)}) %reduce-scatter.13.cloned.1.call-update) | async-done | bytes 2064
  553.9 70.6 %reduce-scatter.7.cloned.1.call-done = bf16[4,256,128]{2,1,0:T(8,128)(2,1)} async-done(((bf16[4,2048,128]{2,1,0:T(8,128)(2,1)}), bf16[4,256,128]{2,1,0:T(8,128)(2,1)}) %reduce-scatter.7.cloned.1.call-update) | async-done | bytes 262160 | tf_op jit(solution)/shard_map/reduce_scatter | solution.py:100
  624.6 1.2 fusion.54
  625.9 1.9 convolution_convert_fusion.4
  629.8 22.2 %reduce-scatter.9.cloned.1.call-done = bf16[256,512]{0,1:T(8,128)(2,1)} async-done(((bf16[256,2048]{0,1:T(8,128)(2,1)}), bf16[256,512]{0,1:T(8,128)(2,1)}) %reduce-scatter.9.cloned.1.call-update) | async-done | bytes 262160 | tf_op jit(solution)/shard_map/reduce_scatter | solution.py:122
  651.9 1.2 fusion.45
  653.1 5.8 psum.15
  659.7 17.4 %all-gather.4.cloned.1.call-done = bf16[256,2048]{0,1:T(8,128)(2,1)} async-done(((bf16[256,512]{0,1:T(8,128)(2,1)}), bf16[256,2048]{0,1:T(8,128)(2,1)}) %all-gather.4.cloned.1.call-update) | async-done | bytes 1048592 | tf_op jit(solution)/shard_map/all_gather | solution.py:131
  677.1 3.4 convolution_convert_fusion.6
  680.7 3.0 convolution_convert_fusion.5
  686.5 7.2 fusion.41
  694.4 35.4 %all-gather.6.cloned.1.call-done = bf16[2048,512]{1,0:T(8,128)(2,1)} async-done(((bf16[256,512]{1,0:T(8,128)(2,1)}), bf16[2048,512]{1,0:T(8,128)(2,1)}) %all-gather.6.cloned.1.call-update) | async-done | bytes 2097168 | tf_op jit(solution)/shard_map/all_gather | solution.py:150
  729.8 49.8 %all-gather.8.cloned.1.call-done = bf16[2048,512]{1,0:T(8,128)(2,1)} async-done(((bf16[256,512]{1,0:T(8,128)(2,1)}), bf16[2048,512]{1,0:T(8,128)(2,1)}) %all-gather.8.cloned.1.call-update) | async-done | bytes 2097168 | tf_op jit(solution)/shard_map/all_gather | solution.py:151
  779.6 49.9 %conditional.1 = (f32[4,256]{1,0:T(4,128)S(1)}, f32[4,256,128]{1,2,0:T(8,128)}) conditional(s32[]{:T(128)} %convert_element_type.119, () %tuple.18, (s32[2048]{0:T(1024)S(1)}, s32[256]{0:T(256)S(1)}, bf16[256,512]{1,0:T(8,128)(2,1)S(1)}, bf16[2048,512]{1,0:T(8,128)(2,1)}, s32[2048]{0:T(1024)S(1)}, /*index=5*/s32[2048]{0:T(1024)S(1)}, ...), branch_computations={%region_13.14_spmd, %region_14.17_spmd} | conditional | flops 1107840000 | bytes 107811880 | solution.py:181
  780.0 3.5 fusion.4
  783.5 2.5 fusion.5
  786.7 22.2 %gather_fusion = f32[2048,4,256]{2,1,0:T(4,128)} fusion(f32[4,256,2048]{1,0,2:T(4,128)} %get-tuple-element.76, s32[2048]{0:T(1024)S(1)} %fusion.17), kind=kCustom, calls=%fused_computation | custom fusion | bytes 16785408 | tf_op jit(solution)/shard_map/cond/branch_1_fun/jit(_take)/gather | solution.py:170
  808.9 9.9 %copy.43 = f32[2048,4,256]{0,2,1:T(8,128)} copy(f32[2048,4,256]{2,1,0:T(4,128)} %gather_fusion) | data formatting | bytes 16777216 | tf_op jit(solution)/shard_map/cond/branch_1_fun/jit(_take)/gather | solution.py:170
  818.8 10.7 %fusion.6 = f32[4,256,128]{1,2,0:T(8,128)} fusion(f32[2048,4,256]{0,2,1:T(8,128)} %copy.43, f32[4,256,2048]{2,1,0:T(8,128)} %copy-done.2, f32[4,256]{1,0:T(4,128)S(1)} %broadcast_maximum_fusion, pred[2048]{0:T(1024)(128)(4,1)S(1)} %compare_and_fusion, pred[256,2048]{1,0:T(8,128)(4,1)S(1)} %broadcast_compare_fusion, bf16[2048,512]{1,0:T(8,128)(2,1)} %get-tuple-element.78), kind=kOutput, calls=%fused_computation.9 | convolution fusion | flops 553648128 | bytes 19929088 | tf_op jit(solution)/shard_map/cond | solution.py:181
  829.5 1.2 divide_convert_fusion
  830.8 3.5 convolution_convert_fusion.3
  834.3 23.5 %reduce-scatter.11.cloned.1.call-done = bf16[256,512]{0,1:T(8,128)(2,1)} async-done(((bf16[256,2048]{0,1:T(8,128)(2,1)}), bf16[256,512]{0,1:T(8,128)(2,1)}) %reduce-scatter.11.cloned.1.call-update) | async-done | bytes 262160 | tf_op jit(solution)/shard_map/reduce_scatter | solution.py:189
  857.8 1.7 fusion.47
  859.5 1.8 copy.57
  (94 shorter events, 14.6 us)
Async XLA Ops:
  6.5 12.2 %copy-start = (bf16[2048,512]{1,0:T(8,128)(2,1)S(1)}, bf16[2048,512]{1,0:T(8,128)(2,1)}, u32[]{:S(2)}) copy-start(bf16[2048,512]{1,0:T(8,128)(2,1)} %param.17) | copy-start | bytes 6291460
  6.5 185.3 %all-reduce.2.cloned.1.call-start = ((), (), s32[]{:S(2)}) async-start(), calls=%async_computation.4 | async-start | bytes 8388608 | tf_op jit(solution)/shard_map/psum | solution.py:13
  32.6 520.4 %reduce-scatter.13.cloned.1.call-start = ((), (), s32[]{:S(2)}) async-start(), calls=%async_computation.11 | async-start | bytes 589824
  231.7 11.0 %copy-start.3 = (bf16[2048,4,128]{2,0,1:T(8,128)(2,1)S(1)}, bf16[2048,4,128]{2,0,1:T(8,128)(2,1)}, u32[]{:S(2)}) copy-start(bf16[2048,4,128]{2,0,1:T(8,128)(2,1)} %get-tuple-element.278) | copy-start | bytes 6291460 | tf_op jit(solution)/shard_map/while
  295.2 11.0 %copy-start.3 = (bf16[2048,4,128]{2,0,1:T(8,128)(2,1)S(1)}, bf16[2048,4,128]{2,0,1:T(8,128)(2,1)}, u32[]{:S(2)}) copy-start(bf16[2048,4,128]{2,0,1:T(8,128)(2,1)} %get-tuple-element.278) | copy-start | bytes 6291460 | tf_op jit(solution)/shard_map/while
  358.7 11.0 %copy-start.3 = (bf16[2048,4,128]{2,0,1:T(8,128)(2,1)S(1)}, bf16[2048,4,128]{2,0,1:T(8,128)(2,1)}, u32[]{:S(2)}) copy-start(bf16[2048,4,128]{2,0,1:T(8,128)(2,1)} %get-tuple-element.278) | copy-start | bytes 6291460 | tf_op jit(solution)/shard_map/while
  422.2 11.0 %copy-start.3 = (bf16[2048,4,128]{2,0,1:T(8,128)(2,1)S(1)}, bf16[2048,4,128]{2,0,1:T(8,128)(2,1)}, u32[]{:S(2)}) copy-start(bf16[2048,4,128]{2,0,1:T(8,128)(2,1)} %get-tuple-element.278) | copy-start | bytes 6291460 | tf_op jit(solution)/shard_map/while
  492.9 131.6 %reduce-scatter.7.cloned.1.call-start = ((), (), s32[]{:S(2)}) async-start(), calls=%async_computation.5 | async-start | bytes 2359296 | tf_op jit(solution)/shard_map/reduce_scatter | solution.py:100
  493.0 132.9 %copy-start.4 = (bf16[512,2048]{1,0:T(8,128)(2,1)S(1)}, bf16[512,2048]{1,0:T(8,128)(2,1)}, u32[]{:S(2)}) copy-start(bf16[512,2048]{1,0:T(8,128)(2,1)} %param.20) | copy-start | bytes 6291460
  497.2 154.7 %reduce-scatter.9.cloned.1.call-start = ((), (), s32[]{:S(2)}) async-start(), calls=%async_computation.6 | async-start | bytes 1310720 | tf_op jit(solution)/shard_map/reduce_scatter | solution.py:122
  627.9 49.3 %all-gather.4.cloned.1.call-start = ((), (), s32[]{:S(2)}) async-start(), calls=%async_computation.7 | async-start | bytes 1310720 | tf_op jit(solution)/shard_map/all_gather | solution.py:131
  659.7 70.2 %all-gather.6.cloned.1.call-start = ((), (), s32[]{:S(2)}) async-start(), calls=%async_computation.8 | async-start | bytes 2359296 | tf_op jit(solution)/shard_map/all_gather | solution.py:150
  677.1 3.5 copy-start.6
  680.6 99.0 %all-gather.8.cloned.1.call-start = ((), (), s32[]{:S(2)}) async-start(), calls=%async_computation.9 | async-start | bytes 2359296 | tf_op jit(solution)/shard_map/all_gather | solution.py:151
  683.7 174.1 %reduce-scatter.11.cloned.1.call-start = ((), (), s32[]{:S(2)}) async-start(), calls=%async_computation.10 | async-start | bytes 1310720 | tf_op jit(solution)/shard_map/reduce_scatter | solution.py:189
  686.5 7.2 copy-start.5
  686.5 7.2 copy-start.7
  783.5 3.2 copy-start.2
  829.5 31.8 %copy-start.1 = (bf16[2048,512]{1,0:T(8,128)(2,1)S(1)}, bf16[2048,512]{1,0:T(8,128)(2,1)}, u32[]{:S(2)}) copy-start(bf16[2048,512]{1,0:T(8,128)(2,1)} %param.17) | copy-start | bytes 6291460
Sparse Core Ops, SparseCore 0:
  32.7 159.0 all-reduce.1
  493.1 59.9 reduce-scatter.12
  556.6 67.9 reduce-scatter.6
  628.0 23.9 reduce-scatter.8
  659.8 17.3 all-gather.3
  680.7 49.0 all-gather.5
  732.0 47.6 all-gather.7
  834.4 23.3 reduce-scatter.10
where the time goes:
time: 877 us; the launch traced here: 868 us
  waiting for transfers between devices  411 us (47%)
  local copies, waits for them, and re-layouts  173 us (20%)
  matrix products  160 us (18%)
  other arithmetic  66.6 us (8%)
  blocking collectives  40.6 us (5%)
  between operations  14.6 us (2%)
    psum x1, waiting for transfers between devices, from_root(): return lax.psum(kept, axis)  136 us
    shift_right_arithmetic x14, local copies, waits for them, and re-layouts, unpack_bits(): jnp.right_shift(packed_words[..., None, :], shifts[:, None])  108 us
    reduce_scatter x1, waiting for transfers between devices, per_device(): lax.psum_scatter((summed * factor[..., None]).astype(jnp.bfloat16), 'seq'...  70.6 us
    dot_general x4, matrix products, cross_block(): jnp.einsum('hqk,khd->hqd', weights, value_heads, preferred_element_type=j...  61.8 us
    unnamed x9, waiting for transfers between devices  55.9 us
    all_gather x1, waiting for transfers between devices, per_device(): value_piece = lax.all_gather(latent_values, 'seq', axis=0, tiled=True)  49.8 us
    dot_general x4, matrix products, cross_block(): jnp.einsum('qhd,khd->hqk', query_block, key_heads, preferred_element_type...  43.7 us
    all_gather x1, waiting for transfers between devices, per_device(): key_piece = lax.all_gather(latent_keys, 'seq', axis=0, tiled=True)  35.4 us
  transfers between devices with their start and end apart: 8, of which 8 were waited for; matrix products, arithmetic and copies ran while one was open for 5% of the time, Pallas kernels for 0%

commit v1 on v0

--- a/solution.py
+++ b/solution.py
@@ -3,14 +3,20 @@
 import jax.numpy as jnp
 from jax import lax
 from jax.sharding import PartitionSpec as P
+from jax.lax import all_gather
 
 keep_scale = 8.0 / 7.0
 masked = -1e30
 
 
+def circles_search(own_rows, net_axis):
+    y1 = all_gather(own_rows, net_axis)
+    return jnp.sum(y1, 0)
+
+
 def from_root(value, axis, source):
     kept = jnp.where(lax.axis_index(axis) == source, value, 0).astype(value.dtype)
-    return lax.psum(kept, axis)
+    return circles_search(kept, axis)
 
 
 def unpack_bits(packed_words, word_bits):

time: 877 us -> 1370 us (1.56)
  waiting for transfers between devices: 411 us -> 883 us
  other arithmetic: 66.6 us -> 81.9 us
    all_gather x0 -> x1, waiting for transfers between devices: none -> 616 us  [circles_search(): y1 = all_gather(own_rows, net_axis)]
    psum x1 -> x0, waiting for transfers between devices: 136 us -> none  [from_root(): return lax.psum(kept, axis)]
    reduce_sum x0 -> x1, other arithmetic: none -> 14.1 us  [circles_search(): return jnp.sum(y1, 0)]
    shift_right_arithmetic x14 -> x15, local copies, waits for them, and re-layouts: 108 us -> 115 us  [unpack_bits(): jnp.right_shift(packed_words[..., None, :], shifts[:, None])]
  transfers between devices with their start and end apart: 8 -> 8, of which waited for: 8 -> 8; matrix products, arithmetic and copies ran while one was open for 5% -> 4% of each run, Pallas kernels for 0% -> 0%
where the time goes in v1:
time: 1370 us; the launch traced here: 1360 us
  waiting for transfers between devices  883 us (64%)
  local copies, waits for them, and re-layouts  184 us (13%)
  matrix products  154 us (11%)
  other arithmetic  81.9 us (6%)
  blocking collectives  41.7 us (3%)
  between operations  14.6 us (1%)
    all_gather x1, waiting for transfers between devices, circles_search(): y1 = all_gather(own_rows, net_axis)  616 us
    shift_right_arithmetic x15, local copies, waits for them, and re-layouts, unpack_bits(): jnp.right_shift(packed_words[..., None, :], shifts[:, None])  115 us
    reduce_scatter x1, waiting for transfers between devices, per_device(): lax.psum_scatter((summed * factor[..., None]).astype(jnp.bfloat16), 'seq'...  70.5 us
    dot_general x4, matrix products, cross_block(): jnp.einsum('hqk,khd->hqd', weights, value_heads, preferred_element_type=j...  61.8 us
    unnamed x9, waiting for transfers between devices  56.3 us
    all_gather x1, waiting for transfers between devices, per_device(): value_piece = lax.all_gather(latent_values, 'seq', axis=0, tiled=True)  49.8 us
    dot_general x4, matrix products, cross_block(): jnp.einsum('qhd,khd->hqk', query_block, key_heads, preferred_element_type...  37.4 us
    pmax x1, blocking collectives, per_device(): row_peak = lax.pmax(row_top, 'seq')  36 us
  transfers between devices with their start and end apart: 8, of which 8 were waited for; matrix products, arithmetic and copies ran while one was open for 4% of the time, Pallas kernels for 0%

profile of v1, /device:TPU:0, one launch (start us, length us, event | category | flops | bytes accessed | tf_op | source)
XLA Modules:
  0.0 1363.0 jit_solution(18334447205237048901)
XLA Ops:
  6.5 5.2 fusion.35
  11.8 3.1 constant_dynamic-slice_fusion.3
  14.9 3.9 copy.37
  18.8 9.7 fusion.40
  28.5 4.1 maximum_select_fusion
  32.6 6.4 copy.38
  39.4 9.0 convolution_convert_fusion.1
  48.4 3.0 copy.42
  51.4 9.3 convolution_convert_fusion
  60.7 2.5 copy.44
  63.2 616.3 %all-gather.5.cloned.1.call-done = bf16[8,2048,1024]{2,1,0:T(8,128)(2,1)} async-done(((bf16[1,2048,1024]{2,1,0:T(8,128)(2,1)}), bf16[8,2048,1024]{2,1,0:T(8,128)(2,1)}) %all-gather.5.cloned.1.call-update) | async-done | bytes 33554448 | tf_op jit(solution)/shard_map/all_gather | solution.py:13
  679.5 14.1 %reduce_sum.49 = bf16[2048,1024]{1,0:T(8,128)(2,1)} reduce(bf16[8,2048,1024]{2,1,0:T(8,128)(2,1)} %all-gather.5.cloned.1.call-done, bf16[]{:T(256)} %constant.99.clone.1), dimensions={0}, to_apply=%region_1.2 | reduce | flops 14680064 | bytes 37748736 | tf_op jit(solution)/shard_map/reduce_sum | solution.py:14
  693.7 3.8 fusion.58
  697.5 2.0 reshape.193
  699.5 253.0 %while.15 = (s32[]{:T(128)}, f32[4,4,512,128]{3,2,0,1:T(8,128)}, f32[4,4,512]{2,1,0:T(4,128)S(1)}, f32[4,4,512]{2,1,0:T(4,128)S(1)}, s32[4]{0:T(128)S(1)}, /*ind...) while((s32[]{:T(128)}, f32[4,4,512,128]{3,2,0,1:T(8,128)}, ...), condition=%wide.region_5.6_spmd.clone, body=%wide.region_2.5_spmd.clone.sunk | while | flops 2224028160 | bytes 143249616 | solution.py:96
  699.7 1.7 dynamic-slice_bitcast_fusion.2
  701.4 7.1 shift_right_arithmetic.115
  708.5 18.0 %shift_right_arithmetic.116 = s32[4,512,2048]{2,1,0:T(8,128)} reshape(s32[4,512,8,256]{3,2,1,0:T(8,128)} %shift_right_arithmetic.115) | data formatting | bytes 33554432 | tf_op jit(solution)/shard_map/while/body/eval_jaxpr/shift_right_arithmetic | solution.py:24
  729.7 9.3 fusion.84
  739.0 15.4 %fusion.85 = f32[4,4,512,128]{3,2,0,1:T(8,128)} fusion(f32[4,4,512,128]{3,2,0,1:T(8,128)} %get-tuple-element.258, s32[]{:T(128)S(6)} %copy.102, bf16[2048,4,128]{2,0,1:T(8,128)(2,1)S(1)} %copy-done.3, s32[4,512,2048]{2,1,0:T(8,128)} %shift_right_arithmetic.116, f32[4,512,2048]{2,1,0:T(8,128)} %get-tuple-element.240, s32[2048]{0:T(1024)S(1)} %bitcast.150, ...), kind=kOutput, calls=%fused_computation.40.clone.1 | convolution fusion | flops 1115684864 | bytes 37765124 | tf_op jit(solution)/shard_map/while/body/eval_jaxpr/hqk,khd->hqd/dot_general | solution.py:91
  754.5 8.4 fusion.86
  762.9 1.7 dynamic-slice_bitcast_fusion.2
  764.6 7.1 shift_right_arithmetic.115
  771.7 18.0 %shift_right_arithmetic.116 = s32[4,512,2048]{2,1,0:T(8,128)} reshape(s32[4,512,8,256]{3,2,1,0:T(8,128)} %shift_right_arithmetic.115) | data formatting | bytes 33554432 | tf_op jit(solution)/shard_map/while/body/eval_jaxpr/shift_right_arithmetic | solution.py:24
  792.9 9.3 fusion.84
  802.2 15.5 %fusion.85 = f32[4,4,512,128]{3,2,0,1:T(8,128)} fusion(f32[4,4,512,128]{3,2,0,1:T(8,128)} %get-tuple-element.258, s32[]{:T(128)S(6)} %copy.102, bf16[2048,4,128]{2,0,1:T(8,128)(2,1)S(1)} %copy-done.3, s32[4,512,2048]{2,1,0:T(8,128)} %shift_right_arithmetic.116, f32[4,512,2048]{2,1,0:T(8,128)} %get-tuple-element.240, s32[2048]{0:T(1024)S(1)} %bitcast.150, ...), kind=kOutput, calls=%fused_computation.40.clone.1 | convolution fusion | flops 1115684864 | bytes 37765124 | tf_op jit(solution)/shard_map/while/body/eval_jaxpr/hqk,khd->hqd/dot_general | solution.py:91
  817.7 8.4 fusion.86
  826.1 1.7 dynamic-slice_bitcast_fusion.2
  827.8 7.1 shift_right_arithmetic.115
  835.0 18.0 %shift_right_arithmetic.116 = s32[4,512,2048]{2,1,0:T(8,128)} reshape(s32[4,512,8,256]{3,2,1,0:T(8,128)} %shift_right_arithmetic.115) | data formatting | bytes 33554432 | tf_op jit(solution)/shard_map/while/body/eval_jaxpr/shift_right_arithmetic | solution.py:24
  856.1 9.4 fusion.84
  865.5 15.4 %fusion.85 = f32[4,4,512,128]{3,2,0,1:T(8,128)} fusion(f32[4,4,512,128]{3,2,0,1:T(8,128)} %get-tuple-element.258, s32[]{:T(128)S(6)} %copy.102, bf16[2048,4,128]{2,0,1:T(8,128)(2,1)S(1)} %copy-done.3, s32[4,512,2048]{2,1,0:T(8,128)} %shift_right_arithmetic.116, f32[4,512,2048]{2,1,0:T(8,128)} %get-tuple-element.240, s32[2048]{0:T(1024)S(1)} %bitcast.150, ...), kind=kOutput, calls=%fused_computation.40.clone.1 | convolution fusion | flops 1115684864 | bytes 37765124 | tf_op jit(solution)/shard_map/while/body/eval_jaxpr/hqk,khd->hqd/dot_general | solution.py:91
  880.9 8.4 fusion.86
  889.3 1.7 dynamic-slice_bitcast_fusion.2
  891.0 7.1 shift_right_arithmetic.115
  898.2 18.0 %shift_right_arithmetic.116 = s32[4,512,2048]{2,1,0:T(8,128)} reshape(s32[4,512,8,256]{3,2,1,0:T(8,128)} %shift_right_arithmetic.115) | data formatting | bytes 33554432 | tf_op jit(solution)/shard_map/while/body/eval_jaxpr/shift_right_arithmetic | solution.py:24
  919.3 9.3 fusion.84
  928.7 15.4 %fusion.85 = f32[4,4,512,128]{3,2,0,1:T(8,128)} fusion(f32[4,4,512,128]{3,2,0,1:T(8,128)} %get-tuple-element.258, s32[]{:T(128)S(6)} %copy.102, bf16[2048,4,128]{2,0,1:T(8,128)(2,1)S(1)} %copy-done.3, s32[4,512,2048]{2,1,0:T(8,128)} %shift_right_arithmetic.116, f32[4,512,2048]{2,1,0:T(8,128)} %get-tuple-element.240, s32[2048]{0:T(1024)S(1)} %bitcast.150, ...), kind=kOutput, calls=%fused_computation.40.clone.1 | convolution fusion | flops 1115684864 | bytes 37765124 | tf_op jit(solution)/shard_map/while/body/eval_jaxpr/hqk,khd->hqd/dot_general | solution.py:91
  944.1 8.4 fusion.86
  952.5 36.0 %pmax.7 = f32[4,2048]{1,0:T(4,128)S(1)} all-reduce(f32[4,2048]{1,0:T(4,128)S(1)} %bitcast.151), channel_id=1, replica_groups=mesh['seq'=8,'head'=4] {'seq'}, use_global_device_ids=true, to_apply=%region_6.7 | all-reduce | flops 8192 | bytes 65536 | tf_op jit(solution)/shard_map/pmax | solution.py:103
  989.6 4.0 fusion.39
  993.7 56.1 %reduce-scatter.13.cloned.1.call-done = bf16[256,4]{1,0:T(8,128)(2,1)} async-done(((bf16[2048,4]{1,0:T(8,128)(2,1)}), bf16[256,4]{1,0:T(8,128)(2,1)}) %reduce-scatter.13.cloned.1.call-update) | async-done | bytes 2064
  1050.8 70.5 %reduce-scatter.7.cloned.1.call-done = bf16[4,256,128]{2,1,0:T(8,128)(2,1)} async-done(((bf16[4,2048,128]{2,1,0:T(8,128)(2,1)}), bf16[4,256,128]{2,1,0:T(8,128)(2,1)}) %reduce-scatter.7.cloned.1.call-update) | async-done | bytes 262160 | tf_op jit(solution)/shard_map/reduce_scatter | solution.py:106
  1122.6 1.8 convolution_convert_fusion.4
  1125.7 2.2 shift_right_arithmetic.62
  1127.9 5.1 shift_right_arithmetic.63
  1133.0 1.4 fusion.42
  1134.4 14.1 %reduce-scatter.9.cloned.1.call-done = bf16[256,512]{1,0:T(8,128)(2,1)} async-done(((bf16[256,2048]{1,0:T(8,128)(2,1)}), bf16[256,512]{1,0:T(8,128)(2,1)}) %reduce-scatter.9.cloned.1.call-update) | async-done | bytes 262160 | tf_op jit(solution)/shard_map/reduce_scatter | solution.py:128
  1149.7 5.8 psum.7
  1156.3 17.4 %all-gather.7.cloned.1.call-done = bf16[256,2048]{1,0:T(8,128)(2,1)} async-done(((bf16[256,512]{1,0:T(8,128)(2,1)}), bf16[256,2048]{1,0:T(8,128)(2,1)}) %all-gather.7.cloned.1.call-update) | async-done | bytes 1048592 | tf_op jit(solution)/shard_map/all_gather | solution.py:137
  1173.8 3.3 convolution_convert_fusion.6
  1177.2 3.3 convolution_convert_fusion.5
  1183.3 7.2 fusion.38
  1191.3 35.1 %all-gather.9.cloned.1.call-done = bf16[2048,512]{1,0:T(8,128)(2,1)} async-done(((bf16[256,512]{1,0:T(8,128)(2,1)}), bf16[2048,512]{1,0:T(8,128)(2,1)}) %all-gather.9.cloned.1.call-update) | async-done | bytes 2097168 | tf_op jit(solution)/shard_map/all_gather | solution.py:156
  1226.4 49.8 %all-gather.11.cloned.1.call-done = bf16[2048,512]{1,0:T(8,128)(2,1)} async-done(((bf16[256,512]{1,0:T(8,128)(2,1)}), bf16[2048,512]{1,0:T(8,128)(2,1)}) %all-gather.11.cloned.1.call-update) | async-done | bytes 2097168 | tf_op jit(solution)/shard_map/all_gather | solution.py:157
  1276.1 49.9 %conditional.1 = (f32[4,256]{1,0:T(4,128)S(1)}, f32[4,256,128]{1,2,0:T(8,128)}) conditional(s32[]{:T(128)} %convert_element_type.121, () %tuple.18, (s32[2048]{0:T(1024)S(1)}, s32[256]{0:T(256)S(1)}, bf16[256,512]{1,0:T(8,128)(2,1)S(1)}, bf16[2048,512]{1,0:T(8,128)(2,1)}, s32[2048]{0:T(1024)S(1)}, /*index=5*/s32[2048]{0:T(1024)S(1)}, ...), branch_computations={%region_13.14_spmd, %region_14.17_spmd} | conditional | flops 1107840000 | bytes 107811880 | solution.py:187
  1276.5 3.5 fusion.4
  1280.0 2.5 fusion.5
  1283.2 22.2 %gather_fusion = f32[2048,4,256]{2,1,0:T(4,128)} fusion(f32[4,256,2048]{1,0,2:T(4,128)} %get-tuple-element.76, s32[2048]{0:T(1024)S(1)} %fusion.17), kind=kCustom, calls=%fused_computation | custom fusion | bytes 16785408 | tf_op jit(solution)/shard_map/cond/branch_1_fun/jit(_take)/gather | solution.py:176
  1305.4 9.9 copy.35
  1315.4 10.7 fusion.6
  1327.3 3.3 convolution_convert_fusion.3
  1330.6 23.5 %reduce-scatter.11.cloned.1.call-done = bf16[256,512]{1,0:T(8,128)(2,1)} async-done(((bf16[256,2048]{1,0:T(8,128)(2,1)}), bf16[256,512]{1,0:T(8,128)(2,1)}) %reduce-scatter.11.cloned.1.call-update) | async-done | bytes 262160 | tf_op jit(solution)/shard_map/reduce_scatter | solution.py:195
  1354.1 1.8 fusion.45
  (96 shorter events, 22.5 us)
Async XLA Ops:
  6.5 12.3 copy-start
  6.5 673.0 %all-gather.5.cloned.1.call-start = ((), (), s32[]{:S(2)}) async-start(), calls=%async_computation.4 | async-start | bytes 37748736 | tf_op jit(solution)/shard_map/all_gather | solution.py:13
  39.0 1010.8 %reduce-scatter.13.cloned.1.call-start = ((), (), s32[]{:S(2)}) async-start(), calls=%async_computation.11 | async-start | bytes 589824
  729.7 9.4 copy-start.3
  792.9 9.4 copy-start.3
  856.1 9.4 copy-start.3
  919.3 9.4 copy-start.3
  989.6 131.7 %reduce-scatter.7.cloned.1.call-start = ((), (), s32[]{:S(2)}) async-start(), calls=%async_computation.5 | async-start | bytes 2359296 | tf_op jit(solution)/shard_map/reduce_scatter | solution.py:106
  989.6 132.9 %copy-start.4 = (bf16[512,2048]{1,0:T(8,128)(2,1)S(1)}, bf16[512,2048]{1,0:T(8,128)(2,1)}, u32[]{:S(2)}) copy-start(bf16[512,2048]{1,0:T(8,128)(2,1)} %param.20) | copy-start | bytes 6291460
  993.7 154.8 %reduce-scatter.9.cloned.1.call-start = ((), (), s32[]{:S(2)}) async-start(), calls=%async_computation.6 | async-start | bytes 1310720 | tf_op jit(solution)/shard_map/reduce_scatter | solution.py:128
  1124.4 49.4 %all-gather.7.cloned.1.call-start = ((), (), s32[]{:S(2)}) async-start(), calls=%async_computation.7 | async-start | bytes 1310720 | tf_op jit(solution)/shard_map/all_gather | solution.py:137
  1156.3 70.1 %all-gather.9.cloned.1.call-start = ((), (), s32[]{:S(2)}) async-start(), calls=%async_computation.8 | async-start | bytes 2359296 | tf_op jit(solution)/shard_map/all_gather | solution.py:156
  1177.1 99.0 %all-gather.11.cloned.1.call-start = ((), (), s32[]{:S(2)}) async-start(), calls=%async_computation.9 | async-start | bytes 2359296 | tf_op jit(solution)/shard_map/all_gather | solution.py:157
  1180.5 173.6 %reduce-scatter.11.cloned.1.call-start = ((), (), s32[]{:S(2)}) async-start(), calls=%async_computation.10 | async-start | bytes 1310720 | tf_op jit(solution)/shard_map/reduce_scatter | solution.py:195
  1183.3 7.2 copy-start.5
  1183.3 7.2 copy-start.6
  1280.0 3.2 copy-start.2
  1326.1 29.8 %copy-start.1 = (bf16[2048,512]{1,0:T(8,128)(2,1)S(1)}, bf16[2048,512]{1,0:T(8,128)(2,1)}, u32[]{:S(2)}) copy-start(bf16[2048,512]{1,0:T(8,128)(2,1)} %param.17) | copy-start | bytes 6291460
Sparse Core Ops, SparseCore 0:
  39.1 640.3 all-gather.4
  989.7 60.1 reduce-scatter.12
  1053.4 67.8 reduce-scatter.6
  1124.5 23.8 reduce-scatter.8
  1156.4 17.3 all-gather.6
  1177.2 49.0 all-gather.8
  1228.5 47.6 all-gather.10
  1330.8 23.3 reduce-scatter.10
